TPU v7x, 32 devices: a whole 2x2x4 slice. The times are simulated.
32 devices in a mesh: row: 4 (over y, x), col: 8 (over z, core).
Axes of the slice: x: 2, y: 2, z: 4, core: 2. Of those that a mesh axis runs over, the one named last changes fastest.
Arguments:
- boundary_start: float32 [16384, 128], P('row'), may hold values from -6 to 6
- volume_start: float32 [256, 512, 128], P(('row', 'col')), may hold values from -6 to 6
- diag_part: float32 [16384], P(('row', 'col')), may hold values from 1 to 2
- incident: float32 [16384, 128], P(('row', 'col')), may hold values from -6 to 6
- kernel: float32 [16384, 16384], P('row', 'col'), may hold values from -0.015625 to 0.015625
- elem_mats: float32 [256, 512, 512], P(('row', 'col')), may hold values from -0.078125 to 0.078125
- trace_owner: int32 [16384, 1], replicated, may hold values from 0 to 31; in each aligned block of 512 rows (0 to 511, 512 to 1023, ...) at most 32 rows name the same one
- trace_slot: int32 [16384], replicated, may hold values from 0 to 4095
- return_owner: int32 [16384, 1], replicated, may hold values from 0 to 31; in each aligned block of 512 rows (0 to 511, 512 to 1023, ...) at most 32 rows name the same one
- return_slot: int32 [16384], replicated, may hold values from 0 to 4095
- face_match: int32 [256, 64], P(('row', 'col')), may hold values from 0 to 63, each once within a row
Outputs:
- boundary_final: float32 [16384, 128], P('row')
- volume_final: float32 [256, 512, 128], P(('row', 'col'))
Inputs may be any that keep to these rules, and one draw needn't show every extreme that they name: `trace_owner`: in each aligned block of 512 boundary rows (the rows of one device), no device is named more than 32 times; some device is named exactly 32 times in some block. `return_owner`: in each aligned block of 512 boundary rows (the rows of one device), no device is named more than 32 times; some device is named exactly 32 times in some block. `face_match`: each row is a permutation of 0 to 63.
All inputs are finite; a program needn't handle non-finite values.
Results may differ from a plain program's by a relative error of at most 0.0001.
Values sent between devices are 32-bit elements; how exact they have to be, the bound alone decides.
A program may use at most 128 MiB of HBM per device.

v0:
```python
import jax
import jax.numpy as jnp
from jax import lax
from jax.sharding import PartitionSpec as P

ITERS = 3
boundary_step = 0.5
volume_step = 0.6
face_weight = 0.5


def passed_along(block, axis, distance):
    devices = range(lax.axis_size(axis))
    route = [(i - distance, i) for i in devices if i - distance in devices]
    return lax.ppermute(block, axis, route)


def spread(block, axis, holder):
    block = jnp.where(lax.axis_index(axis) == holder, block, jnp.zeros_like(block))
    return lax.psum(block, axis)


def slot_rank(owners):
    row_total = owners.shape[0]
    same_owner = owners[:, None] == owners[None, :]
    positions = jnp.arange(row_total, dtype=jnp.int32)
    earlier = positions[None, :] < positions[:, None]
    return jnp.sum((same_owner & earlier).astype(jnp.int32), axis=1)


def send_plan(owners, rank_rows, devices, capacity):
    positions = jnp.arange(owners.shape[0], dtype=jnp.int32)
    targets = jnp.arange(devices, dtype=jnp.int32)
    places = jnp.arange(capacity, dtype=jnp.int32)
    select = (owners[None, None, :] == targets[:, None, None]) & (
        rank_rows[None, None, :] == places[None, :, None]
    )
    index = jnp.sum(jnp.where(select, positions[None, None, :], 0), axis=2)
    valid_slot = jnp.any(select, axis=2)
    return (index, valid_slot)


def block_plan(owner_blocks, slot_blocks, device_self, capacity):
    mine_rows = owner_blocks == device_self
    rank_rows = jnp.cumsum(mine_rows.astype(jnp.int32), axis=1) - 1
    places = jnp.arange(capacity, dtype=jnp.int32)
    select = mine_rows[:, None, :] & (rank_rows[:, None, :] == places[None, :, None])
    index = jnp.sum(jnp.where(select, slot_blocks[:, None, :], 0), axis=2)
    valid_slot = jnp.any(select, axis=2)
    return (index, valid_slot)


def shards(
    boundary_start,
    volume_start,
    diag_part,
    incident,
    kernel,
    elem_mats,
    trace_owner,
    trace_slot,
    return_owner,
    return_slot,
    face_match,
):
    highest = lax.Precision.HIGHEST
    devices = lax.axis_size(("row", "col"))
    row_devices = lax.axis_size("row")
    col_devices = lax.axis_size("col")
    device_self = lax.axis_index(("row", "col"))
    col_index = lax.axis_index("col")
    total_rows = trace_slot.shape[0]
    share_rows = total_rows // devices
    capacity = max(2, 2 * share_rows // devices)
    panel_length = total_rows // col_devices
    per_panel = col_devices // row_devices
    elem_count, node_count, columns = volume_start.shape
    face_count = face_match.shape[1]
    trace_blocks = trace_owner[:, 0].reshape(devices, share_rows)
    trace_slots = trace_slot.reshape(devices, share_rows)
    return_blocks = return_owner[:, 0].reshape(devices, share_rows)
    return_slots = return_slot.reshape(devices, share_rows)
    trace_send, trace_send_ok = block_plan(trace_blocks, trace_slots, device_self, capacity)
    own_trace = lax.dynamic_index_in_dim(trace_blocks, device_self, 0, keepdims=False)
    trace_pick = own_trace * capacity + slot_rank(own_trace)
    own_return = lax.dynamic_index_in_dim(return_blocks, device_self, 0, keepdims=False)
    flux_send, flux_send_ok = send_plan(own_return, slot_rank(own_return), devices, capacity)
    flux_take, flux_take_ok = block_plan(return_blocks, return_slots, device_self, capacity)
    panel_current = boundary_start
    volume_field = volume_start
    for sweep_index in range(ITERS):
        share_current = lax.dynamic_slice_in_dim(
            panel_current, col_index * share_rows, share_rows, 0
        )
        volume_flat = volume_field.reshape(elem_count * node_count, columns)
        outgoing = jnp.where(trace_send_ok[:, :, None], volume_flat[trace_send], 0.0)
        arrived = lax.all_to_all(outgoing, ("row", "col"), split_axis=0, concat_axis=0, tiled=True)
        traced = arrived.reshape(devices * capacity, columns)[trace_pick]
        leaving = jnp.where(flux_send_ok[:, :, None], share_current[flux_send], 0.0)
        landed = lax.all_to_all(leaving, ("row", "col"), split_axis=0, concat_axis=0, tiled=True)
        landed_rows = jnp.where(flux_take_ok[:, :, None], landed, 0.0).reshape(
            devices * capacity, columns
        )
        flux_field = (
            jnp.zeros_like(volume_flat)
            .at[flux_take.reshape(-1)]
            .add(landed_rows)
            .reshape(volume_field.shape)
        )
        lower_faces = passed_along(volume_field[:, node_count - face_count :, :], ("row", "col"), 1)
        matched = jax.vmap(lambda face_rows, face_order: face_rows[face_order])(
            lower_faces, face_match
        )
        half_panel = lax.dynamic_slice_in_dim(
            panel_current, col_index % per_panel * panel_length, panel_length, 0
        )
        column_values = spread(half_panel, "row", col_index // per_panel)
        local_term = diag_part[:, None] * share_current - incident - traced
        partial_value = jnp.dot(
            kernel, column_values, precision=highest, preferred_element_type=jnp.float32
        )
        row_start = col_index * share_rows
        own_part = lax.dynamic_slice_in_dim(partial_value, row_start, share_rows, 0) + local_term
        partial_value = lax.dynamic_update_slice_in_dim(partial_value, own_part, row_start, 0)
        residual = lax.psum(partial_value, "col")
        panel_current = panel_current - boundary_step * residual
        applied = jnp.einsum("enm,emr->enr", elem_mats, volume_field, precision=highest)
        updated = volume_field - volume_step * (volume_field + applied - flux_field)
        volume_field = updated.at[:, :face_count, :].add(volume_step * face_weight * matched)
    return (panel_current, volume_field)


def solution(mesh):
    placed = (
        P("row", None),
        P(("row", "col"), None, None),
        P(("row", "col")),
        P(("row", "col"), None),
        P("row", "col"),
        P(("row", "col"), None, None),
        P(),
        P(),
        P(),
        P(),
        P(("row", "col"), None),
    )
    return jax.shard_map(
        shards,
        mesh=mesh,
        in_specs=placed,
        out_specs=(P("row", None), P(("row", "col"), None, None)),
        check_vma=False,
    )
```

profile of v0, /device:TPU:0, one launch (start us, length us, event | category | flops | bytes accessed | tf_op | source)
XLA Modules:
  0.0 601.1 jit_solution(13699476681869330466)
XLA Ops:
  7.2 2.9 copy.59
  10.1 2.4 dynamic-slice_select_fusion.2
  17.0 2.8 gather_fusion
  20.9 7.3 %all-to-all-start = ((f32[32,32,128]{2,1,0:T(8,128)}), f32[32,32,128]{2,1,0:T(8,128)S(1)}, u32[]{:S(2)}, u32[]{:S(2)}) async-start(f32[32,32,128]{2,1,0:T(8,128)} %broadcast_select_fusion.8), calls=%async_computation | async-start | bytes 1048576 | tf_op jit(solution)/shard_map/all_to_all | solution.py:97
  28.9 2.7 collective-permute-start
  36.1 8.7 %all-to-all-done = f32[32,32,128]{2,1,0:T(8,128)S(1)} async-done(((f32[32,32,128]{2,1,0:T(8,128)}), f32[32,32,128]{2,1,0:T(8,128)S(1)}, u32[]{:S(2)}, u32[]{:S(2)}) %all-to-all-start) | async-done | bytes 524320 | tf_op jit(solution)/shard_map/all_to_all | solution.py:97
  46.0 23.2 %all-reduce.7.cloned.1.call-done = f32[2048,128]{0,1:T(8,128)} async-done(((f32[2048,128]{0,1:T(8,128)}), f32[2048,128]{0,1:T(8,128)}) %all-reduce.7.cloned.1.call-update) | async-done | bytes 1048592 | tf_op jit(solution)/shard_map/psum | solution.py:20
  69.2 38.4 %fusion.29 = f32[128,4096]{1,0:T(8,128)S(1)} fusion(f32[2048,128]{0,1:T(8,128)} %all-reduce.7.cloned.1.call-done, f32[4096,2048]{1,0:T(8,128)} %param.21), kind=kOutput, calls=%fused_computation.106 | convolution fusion | flops 12884901888 | bytes 36700160 | tf_op jit(solution)/shard_map/dot_general | solution.py:119
  109.3 1.3 copy-done.5
  110.8 2.8 gather_fusion.2
  114.6 4.6 all-to-all-start.1
  120.9 3.7 gather_fusion.9
  124.7 10.8 %all-to-all-done.1 = f32[32,32,128]{2,1,0:T(8,128)S(1)} async-done(((f32[32,32,128]{2,1,0:T(8,128)}), f32[32,32,128]{2,1,0:T(8,128)S(1)}, u32[]{:S(2)}, u32[]{:S(2)}) %all-to-all-start.1) | async-done | bytes 524320 | tf_op jit(solution)/shard_map/all_to_all | solution.py:100
  135.7 8.0 %scatter_custom_fusion = f32[4096,128]{1,0:T(8,128)} fusion(s32[1024]{0:T(1024)S(1)} %bitcast.132, f32[1024,128]{1,0:T(8,128)S(1)} %bitcast.123, f32[]{:T(128)} %constant.143.clone.1), kind=kCustom, calls=%fused_computation.44 | custom fusion | flops 131072 | bytes 2097156 | tf_op jit(solution)/shard_map/scatter-add | solution.py:107
  143.7 11.2 %multiply_subtract_fusion.2 = f32[8,512,128]{2,1,0:T(8,128)S(1)} fusion(f32[8,512,128]{2,1,0:T(8,128)} %param.18, f32[8,512,128]{2,1,0:T(8,128)} %bitcast.112, f32[8,512,512]{2,1,0:T(8,128)} %param.22), kind=kOutput, calls=%fused_computation.28 | convolution fusion | flops 3223322624 | bytes 14680064 | tf_op jit(solution)/shard_map/enm,emr->enr/dot_general | solution.py:127
  155.0 2.8 gather_fusion.3
  157.8 33.4 %all-reduce.9.cloned.1.call-done = f32[4096,128]{0,1:T(8,128)} async-done(((f32[4096,128]{0,1:T(8,128)}), f32[4096,128]{0,1:T(8,128)}) %all-reduce.9.cloned.1.call-update) | async-done | bytes 2097168 | tf_op jit(solution)/shard_map/psum | solution.py:125
  191.2 2.5 multiply_subtract_fusion.3
  196.2 20.6 %all_to_all.30 = f32[32,32,128]{2,1,0:T(8,128)S(1)} all-to-all(f32[32,32,128]{2,1,0:T(8,128)S(1)} %broadcast_select_fusion.5), channel_id=1, replica_groups=mesh['row'=4,'col'=8] {'row','col'}, dimensions={0} | all-to-all | bytes 1048576 | tf_op jit(solution)/shard_map/all_to_all | solution.py:97
  218.1 35.8 %all-reduce.11.cloned.1.call-done = f32[2048,128]{0,1:T(8,128)} async-done(((f32[2048,128]{0,1:T(8,128)}), f32[2048,128]{0,1:T(8,128)}) %all-reduce.11.cloned.1.call-update) | async-done | bytes 1048592 | tf_op jit(solution)/shard_map/psum | solution.py:20
  253.9 39.2 %fusion.30 = f32[128,4096]{1,0:T(8,128)} fusion(f32[2048,128]{0,1:T(8,128)} %all-reduce.11.cloned.1.call-done, f32[4096,2048]{1,0:T(8,128)} %param.21), kind=kOutput, calls=%fused_computation.107 | convolution fusion | flops 12884901888 | bytes 36700160 | tf_op jit(solution)/shard_map/dot_general | solution.py:119
  293.0 1.6 copy.87
  295.8 1.3 copy-done.6
  297.2 2.8 gather_fusion.5
  301.0 4.6 all-to-all-start.3
  305.7 2.2 collective-permute-start.1
  309.0 3.7 gather_fusion.10
  312.8 9.4 %all-to-all-done.3 = f32[32,32,128]{2,1,0:T(8,128)S(1)} async-done(((f32[32,32,128]{2,1,0:T(8,128)}), f32[32,32,128]{2,1,0:T(8,128)S(1)}, u32[]{:S(2)}, u32[]{:S(2)}) %all-to-all-start.3) | async-done | bytes 524320 | tf_op jit(solution)/shard_map/all_to_all | solution.py:100
  322.4 8.1 %scatter_custom_fusion.1 = f32[4096,128]{1,0:T(8,128)} fusion(s32[1024]{0:T(1024)S(1)} %bitcast.133, f32[1024,128]{1,0:T(8,128)S(1)} %bitcast.124, f32[]{:T(128)} %constant.143.clone.1), kind=kCustom, calls=%fused_computation.42 | custom fusion | flops 131072 | bytes 2097156 | tf_op jit(solution)/shard_map/scatter-add | solution.py:107
  330.6 10.9 %fusion.6 = f32[8,512,128]{2,1,0:T(8,128)S(1)} fusion(f32[8,512,128]{2,1,0:T(8,128)} %copy-done, f32[8,512,128]{2,1,0:T(8,128)} %bitcast.111, f32[8,512,512]{2,1,0:T(8,128)} %param.22), kind=kOutput, calls=%fused_computation.25 | convolution fusion | flops 3223322624 | bytes 14680064 | tf_op jit(solution)/shard_map/enm,emr->enr/dot_general | solution.py:127
  341.5 2.8 gather_fusion.6
  344.4 46.2 %all-reduce.13.cloned.1.call-done = f32[4096,128]{0,1:T(8,128)} async-done(((f32[4096,128]{0,1:T(8,128)}), f32[4096,128]{0,1:T(8,128)}) %all-reduce.13.cloned.1.call-update) | async-done | bytes 2097168 | tf_op jit(solution)/shard_map/psum | solution.py:125
  390.5 2.5 multiply_subtract_fusion.1
  395.6 20.3 %all_to_all.31 = f32[32,32,128]{2,1,0:T(8,128)S(1)} all-to-all(f32[32,32,128]{2,1,0:T(8,128)S(1)} %broadcast_select_fusion.2), channel_id=1, replica_groups=mesh['row'=4,'col'=8] {'row','col'}, dimensions={0} | all-to-all | bytes 1048576 | tf_op jit(solution)/shard_map/all_to_all | solution.py:97
  417.0 36.1 %all-reduce.15.cloned.1.call-done = f32[2048,128]{0,1:T(8,128)} async-done(((f32[2048,128]{0,1:T(8,128)}), f32[2048,128]{0,1:T(8,128)}) %all-reduce.15.cloned.1.call-update) | async-done | bytes 1048592 | tf_op jit(solution)/shard_map/psum | solution.py:20
  453.1 39.1 %fusion.31 = f32[128,4096]{1,0:T(8,128)} fusion(f32[2048,128]{0,1:T(8,128)} %all-reduce.15.cloned.1.call-done, f32[4096,2048]{1,0:T(8,128)} %param.21), kind=kOutput, calls=%fused_computation.108 | convolution fusion | flops 12884901888 | bytes 36700160 | tf_op jit(solution)/shard_map/dot_general | solution.py:119
  492.2 1.6 copy.91
  496.4 2.8 gather_fusion.8
  500.2 4.6 all-to-all-start.5
  504.9 2.2 collective-permute-start.2
  508.2 3.7 gather_fusion.11
  511.9 9.5 %all-to-all-done.5 = f32[32,32,128]{2,1,0:T(8,128)S(1)} async-done(((f32[32,32,128]{2,1,0:T(8,128)}), f32[32,32,128]{2,1,0:T(8,128)S(1)}, u32[]{:S(2)}, u32[]{:S(2)}) %all-to-all-start.5) | async-done | bytes 524320 | tf_op jit(solution)/shard_map/all_to_all | solution.py:100
  521.6 8.2 %scatter_custom_fusion.2 = f32[4096,128]{1,0:T(8,128)} fusion(s32[1024]{0:T(1024)S(1)} %bitcast.134, f32[1024,128]{1,0:T(8,128)S(1)} %bitcast.122, f32[]{:T(128)} %constant.143.clone.1), kind=kCustom, calls=%fused_computation.40 | custom fusion | flops 131072 | bytes 2097156 | tf_op jit(solution)/shard_map/scatter-add | solution.py:107
  529.8 10.7 %fusion.3 = f32[8,512,128]{2,1,0:T(8,128)} fusion(f32[8,512,128]{2,1,0:T(8,128)S(1)} %fusion.20, f32[8,512,128]{2,1,0:T(8,128)} %bitcast.110, f32[8,512,512]{2,1,0:T(8,128)} %param.22), kind=kOutput, calls=%fused_computation.21 | convolution fusion | flops 3223322624 | bytes 14680064 | tf_op jit(solution)/shard_map/enm,emr->enr/dot_general | solution.py:127
  540.5 1.7 fusion.19
  542.2 47.5 %all-reduce.17.cloned.1.call-done = f32[4096,128]{0,1:T(8,128)} async-done(((f32[4096,128]{0,1:T(8,128)}), f32[4096,128]{0,1:T(8,128)}) %all-reduce.17.cloned.1.call-update) | async-done | bytes 2097168 | tf_op jit(solution)/shard_map/psum | solution.py:125
  589.7 2.4 multiply_subtract_fusion
  592.2 1.8 copy.73
  (119 shorter events, 32.7 us)
Async XLA Ops:
  7.2 62.0 %all-reduce.7.cloned.1.call-start = ((), (), s32[]{:S(2)}) async-start(), calls=%async_computation.6 | async-start | bytes 2097152 | tf_op jit(solution)/shard_map/psum | solution.py:20
  10.1 2.5 copy-start.8
  10.1 2.5 copy-start.9
  10.1 5.5 copy-start.10
  10.1 6.9 %copy-start.1 = (f32[8,512,128]{2,1,0:T(8,128)S(1)}, f32[8,512,128]{2,1,0:T(8,128)}, u32[]{:S(2)}) copy-start(f32[8,512,128]{2,1,0:T(8,128)} %param.18) | copy-start | bytes 6291460
  19.8 13.8 %copy-start.7 = (f32[512,128]{1,0:T(8,128)S(1)}, f32[512,128]{1,0:T(8,128)}, u32[]{:S(2)}) copy-start(f32[512,128]{1,0:T(8,128)} %param.20) | copy-start | bytes 786436
  19.8 15.4 %copy-start.11 = (s32[16384]{0:T(1024)S(1)}, s32[16384]{0:T(1024)}, u32[]{:S(2)}) copy-start(s32[16384]{0:T(1024)} %param.26) | copy-start | bytes 196612
  20.9 23.9 %all-to-all-start = ((f32[32,32,128]{2,1,0:T(8,128)}), f32[32,32,128]{2,1,0:T(8,128)S(1)}, u32[]{:S(2)}, u32[]{:S(2)}) async-start(f32[32,32,128]{2,1,0:T(8,128)} %broadcast_select_fusion.8), calls=%async_computation | async-start | bytes 1048576 | tf_op jit(solution)/shard_map/all_to_all | solution.py:97
  28.9 92.0 %collective-permute-start = (f32[8,64,128]{2,1,0:T(8,128)}, f32[8,64,128]{2,1,0:T(8,128)S(1)}, u32[]{:S(2)}, u32[]{:S(2)}) collective-permute-start(f32[8,64,128]{2,1,0:T(8,128)} %slice.98), channel_id=1, source_target_pairs={{0,1},{1,2},{2,3},{3,4},{4,5},{5,6},{6,7},{7,8},{8,9},{9,10},{10,1... | collective-permute-start | bytes 786440 | tf_op jit(solution)/shard_map/ppermute | solution.py:15
  107.6 0.7 copy-start.12
  109.3 1.3 copy-start.5
  113.6 6.5 %copy-start.13 = (s32[8,64]{1,0:T(8,128)S(1)}, s32[8,64]{1,0:T(8,128)}, u32[]{:S(2)}) copy-start(s32[8,64]{1,0:T(8,128)} %param.27) | copy-start | bytes 6148
  114.6 20.9 %all-to-all-start.1 = ((f32[32,32,128]{2,1,0:T(8,128)}), f32[32,32,128]{2,1,0:T(8,128)S(1)}, u32[]{:S(2)}, u32[]{:S(2)}) async-start(f32[32,32,128]{2,1,0:T(8,128)} %broadcast_select_fusion.7), calls=%async_computation.1 | async-start | bytes 1048576 | tf_op jit(solution)/shard_map/all_to_all | solution.py:100
  119.2 72.0 %all-reduce.9.cloned.1.call-start = ((), (), s32[]{:S(2)}) async-start(), calls=%async_computation.7 | async-start | bytes 4194304 | tf_op jit(solution)/shard_map/psum | solution.py:125
  124.6 129.2 %all-reduce.11.cloned.1.call-start = ((), (), s32[]{:S(2)}) async-start(), calls=%async_computation.8 | async-start | bytes 2097152 | tf_op jit(solution)/shard_map/psum | solution.py:20
  155.0 150.7 %copy-start = (f32[8,512,128]{2,1,0:T(8,128)}, f32[8,512,128]{2,1,0:T(8,128)S(1)}, u32[]{:S(2)}) copy-start(f32[8,512,128]{2,1,0:T(8,128)S(1)} %fusion.21) | copy-start | bytes 6291460
  193.6 1.3 copy-start.3
  295.8 1.3 copy-start.6
  301.0 21.2 %all-to-all-start.3 = ((f32[32,32,128]{2,1,0:T(8,128)}), f32[32,32,128]{2,1,0:T(8,128)S(1)}, u32[]{:S(2)}, u32[]{:S(2)}) async-start(f32[32,32,128]{2,1,0:T(8,128)} %broadcast_select_fusion.4), calls=%async_computation.3 | async-start | bytes 1048576 | tf_op jit(solution)/shard_map/all_to_all | solution.py:100
  305.6 84.9 %all-reduce.13.cloned.1.call-start = ((), (), s32[]{:S(2)}) async-start(), calls=%async_computation.9 | async-start | bytes 4194304 | tf_op jit(solution)/shard_map/psum | solution.py:125
  305.7 3.3 collective-permute-start.1
  312.7 140.4 %all-reduce.15.cloned.1.call-start = ((), (), s32[]{:S(2)}) async-start(), calls=%async_computation.10 | async-start | bytes 2097152 | tf_op jit(solution)/shard_map/psum | solution.py:20
  393.0 1.3 copy-start.2
  495.0 1.3 copy-start.4
  500.2 21.2 %all-to-all-start.5 = ((f32[32,32,128]{2,1,0:T(8,128)}), f32[32,32,128]{2,1,0:T(8,128)S(1)}, u32[]{:S(2)}, u32[]{:S(2)}) async-start(f32[32,32,128]{2,1,0:T(8,128)} %broadcast_select_fusion.1), calls=%async_computation.5 | async-start | bytes 1048576 | tf_op jit(solution)/shard_map/all_to_all | solution.py:100
  504.8 84.9 %all-reduce.17.cloned.1.call-start = ((), (), s32[]{:S(2)}) async-start(), calls=%async_computation.11 | async-start | bytes 4194304 | tf_op jit(solution)/shard_map/psum | solution.py:125
  504.9 3.3 collective-permute-start.2
Sparse Core Ops, SparseCore 0:
  12.7 56.4 all-reduce.6
  124.8 66.3 all-reduce.8
  196.2 57.6 all-reduce.10
  312.9 77.6 all-reduce.12
  395.5 57.5 all-reduce.14
  512.0 77.6 all-reduce.16
where the time goes:
time: 605 us; the launch traced here: 601 us
  waiting for transfers between devices  263 us (43%)
  matrix products  150 us (25%)
  other arithmetic  55 us (9%)
  local copies, waits for them, and re-layouts  49 us (8%)
  blocking collectives  40.9 us (7%)
  starting transfers between devices  28.6 us (5%)
  between operations  15.1 us (2%)
    psum x3, waiting for transfers between devices, shards(): residual = lax.psum(partial_value, 'col')  127 us
    dot_general x3, matrix products, shards(): jnp.dot(kernel, column_values, precision=highest, preferred_element_type=...  117 us
    psum x3, waiting for transfers between devices, spread(): return lax.psum(block, axis)  95.1 us
    all_to_all x2, blocking collectives, shards(): lax.all_to_all(outgoing, ('row', 'col'), split_axis=0, concat_axis=0, til...  40.9 us
    dot_general x3, matrix products, shards(): jnp.einsum('enm,emr->enr', elem_mats, volume_field, precision=highest)  32.8 us
    all_to_all x3, waiting for transfers between devices, shards(): lax.all_to_all(leaving, ('row', 'col'), split_axis=0, concat_axis=0, tile...  29.7 us
    scatter-add x3, other arithmetic, shards(): flux_field = jnp.zeros_like(volume_flat).at[flux_take.reshape(-1)].add(la...  24.3 us
    unnamed x35, local copies, waits for them, and re-layouts  15.8 us
  transfers between devices with their start and end apart: 13, of which 12 were waited for; matrix products, arithmetic and copies ran while one was open for 23% of the time, Pallas kernels for 0%

commit v1 on v0

--- a/solution.py
+++ b/solution.py
@@ -122,7 +122,13 @@
         row_start = col_index * share_rows
         own_part = lax.dynamic_slice_in_dim(partial_value, row_start, share_rows, 0) + local_term
         partial_value = lax.dynamic_update_slice_in_dim(partial_value, own_part, row_start, 0)
-        residual = lax.psum(partial_value, "col")
+        peers = lax.axis_size("col")
+        residual, stride = (partial_value, 1)
+        while stride < peers:
+            residual = residual + lax.ppermute(
+                residual, "col", [(i_2, i_2 ^ stride) for i_2 in range(peers)]
+            )
+            stride = 2 * stride
         panel_current = panel_current - boundary_step * residual
         applied = jnp.einsum("enm,emr->enr", elem_mats, volume_field, precision=highest)
         updated = volume_field - volume_step * (volume_field + applied - flux_field)

time: 605 us -> 855 us (1.41)
  the two profiles are of different devices: /device:TPU:0 before, /device:TPU:20 now
where the time goes in v1:
time: 855 us; the launch traced here: 846 us
  waiting for transfers between devices  492 us (58%)
  matrix products  149 us (17%)
  other arithmetic  71 us (8%)
  local copies, waits for them, and re-layouts  46.7 us (5%)
  starting transfers between devices  36.2 us (4%)
  blocking collectives  36 us (4%)
  between operations  14.7 us (2%)
    ppermute x9, waiting for transfers between devices, shards(): lax.ppermute(residual, 'col', [(i_2, i_2 ^ stride) for i_2 in range(peers)])  192 us
    ppermute x3, waiting for transfers between devices, passed_along(): return lax.ppermute(block, axis, route)  183 us
    dot_general x3, matrix products, shards(): jnp.dot(kernel, column_values, precision=highest, preferred_element_type=...  117 us
    psum x3, waiting for transfers between devices, spread(): return lax.psum(block, axis)  104 us
    all_to_all x2, blocking collectives, shards(): lax.all_to_all(outgoing, ('row', 'col'), split_axis=0, concat_axis=0, til...  36 us
    dot_general x3, matrix products, shards(): jnp.einsum('enm,emr->enr', elem_mats, volume_field, precision=highest)  31.9 us
    scatter-add x3, other arithmetic, shards(): flux_field = jnp.zeros_like(volume_flat).at[flux_take.reshape(-1)].add(la...  24 us
  transfers between devices with their start and end apart: 19, of which 13 were waited for; matrix products, arithmetic and copies ran while one was open for 14% of the time, Pallas kernels for 0%

profile of v1, /device:TPU:20, one launch (start us, length us, event | category | flops | bytes accessed | tf_op | source)
XLA Modules:
  0.0 846.1 jit_solution(123039404420790050)
XLA Ops:
  7.2 2.9 copy.59
  10.1 2.4 dynamic-slice_select_fusion.2
  17.1 2.8 gather_fusion
  20.9 5.9 all-to-all-start
  27.3 12.6 %all-to-all-done = f32[32,32,128]{2,1,0:T(8,128)S(1)} async-done(((f32[32,32,128]{2,1,0:T(8,128)}), f32[32,32,128]{2,1,0:T(8,128)S(1)}, u32[]{:S(2)}, u32[]{:S(2)}) %all-to-all-start) | async-done | bytes 524320 | tf_op jit(solution)/shard_map/all_to_all | solution.py:97
  41.1 26.3 %all-reduce.4.cloned.1.call-done = f32[2048,128]{0,1:T(8,128)} async-done(((f32[2048,128]{0,1:T(8,128)}), f32[2048,128]{0,1:T(8,128)}) %all-reduce.4.cloned.1.call-update) | async-done | bytes 1048592 | tf_op jit(solution)/shard_map/psum | solution.py:20
  67.4 39.2 %fusion.29 = f32[128,4096]{1,0:T(8,128)} fusion(f32[2048,128]{0,1:T(8,128)} %all-reduce.4.cloned.1.call-done, f32[4096,2048]{1,0:T(8,128)} %param.21), kind=kOutput, calls=%fused_computation.106 | convolution fusion | flops 12884901888 | bytes 36700160 | tf_op jit(solution)/shard_map/dot_general | solution.py:119
  109.4 4.1 collective-permute-done
  116.6 2.1 collective-permute-start.3
  122.9 2.8 gather_fusion.2
  126.7 6.0 all-to-all-start.1
  132.7 33.5 %collective-permute-done.1 = f32[4096,128]{0,1:T(8,128)} collective-permute-done((f32[4096,128]{0,1:T(8,128)}, f32[4096,128]{0,1:T(8,128)}, u32[]{:S(2)}, u32[]{:S(2)}) %collective-permute-start.1) | collective-permute-done | bytes 2097184 | tf_op jit(solution)/shard_map/ppermute | solution.py:128
  166.3 3.8 add.194
  170.1 4.4 collective-permute-start.2
  175.9 3.7 gather_fusion.9
  179.9 7.9 scatter_custom_fusion
  187.8 11.1 %multiply_subtract_fusion.2 = f32[8,512,128]{2,1,0:T(8,128)S(1)} fusion(f32[8,512,128]{2,1,0:T(8,128)} %param.18, f32[8,512,128]{2,1,0:T(8,128)} %bitcast.112, f32[8,512,512]{2,1,0:T(8,128)} %param.22), kind=kOutput, calls=%fused_computation.28 | convolution fusion | flops 3223322624 | bytes 14680064 | tf_op jit(solution)/shard_map/enm,emr->enr/dot_general | solution.py:133
  199.0 2.8 gather_fusion.3
  201.8 60.7 %collective-permute-done.2 = f32[4096,128]{0,1:T(8,128)} collective-permute-done((f32[4096,128]{0,1:T(8,128)}, f32[4096,128]{0,1:T(8,128)}, u32[]{:S(2)}, u32[]{:S(2)}) %collective-permute-start.2) | collective-permute-done | bytes 2097184 | tf_op jit(solution)/shard_map/ppermute | solution.py:128
  262.6 3.2 multiply_subtract_fusion.3
  268.4 19.0 %all_to_all.30 = f32[32,32,128]{2,1,0:T(8,128)S(1)} all-to-all(f32[32,32,128]{2,1,0:T(8,128)S(1)} %broadcast_select_fusion.5), channel_id=1, replica_groups=mesh['row'=4,'col'=8] {'row','col'}, dimensions={0} | all-to-all | bytes 1048576 | tf_op jit(solution)/shard_map/all_to_all | solution.py:97
  288.6 38.8 %all-reduce.6.cloned.1.call-done = f32[2048,128]{0,1:T(8,128)} async-done(((f32[2048,128]{0,1:T(8,128)}), f32[2048,128]{0,1:T(8,128)}) %all-reduce.6.cloned.1.call-update) | async-done | bytes 1048592 | tf_op jit(solution)/shard_map/psum | solution.py:20
  327.4 39.1 %fusion.30 = f32[128,4096]{1,0:T(8,128)} fusion(f32[2048,128]{0,1:T(8,128)} %all-reduce.6.cloned.1.call-done, f32[4096,2048]{1,0:T(8,128)} %param.21), kind=kOutput, calls=%fused_computation.107 | convolution fusion | flops 12884901888 | bytes 36700160 | tf_op jit(solution)/shard_map/dot_general | solution.py:119
  369.3 4.1 collective-permute-done.4
  376.6 2.8 gather_fusion.5
  380.5 4.0 all-to-all-start.3
  384.5 42.7 %collective-permute-done.5 = f32[4096,128]{0,1:T(8,128)} collective-permute-done((f32[4096,128]{0,1:T(8,128)}, f32[4096,128]{0,1:T(8,128)}, u32[]{:S(2)}, u32[]{:S(2)}) %collective-permute-start.5) | collective-permute-done | bytes 2097184 | tf_op jit(solution)/shard_map/ppermute | solution.py:128
  427.3 3.8 add.203
  431.7 1.9 collective-permute-start.7
  433.6 91.6 %collective-permute-done.7 = f32[8,64,128]{2,1,0:T(8,128)S(1)} collective-permute-done((f32[8,64,128]{2,1,0:T(8,128)S(1)}, f32[8,64,128]{2,1,0:T(8,128)S(1)}, u32[]{:S(2)}, u32[]{:S(2)}) %collective-permute-start.7) | collective-permute-done | bytes 262176 | tf_op jit(solution)/shard_map/ppermute | solution.py:15
  525.2 3.7 gather_fusion.10
  529.1 8.0 scatter_custom_fusion.1
  537.2 10.9 %fusion.6 = f32[8,512,128]{2,1,0:T(8,128)S(1)} fusion(f32[8,512,128]{2,1,0:T(8,128)} %copy-done, f32[8,512,128]{2,1,0:T(8,128)} %bitcast.111, f32[8,512,512]{2,1,0:T(8,128)} %param.22), kind=kOutput, calls=%fused_computation.25 | convolution fusion | flops 3223322624 | bytes 14680064 | tf_op jit(solution)/shard_map/enm,emr->enr/dot_general | solution.py:133
  548.1 2.8 gather_fusion.6
  551.0 3.2 multiply_subtract_fusion.1
  556.8 16.9 %all_to_all.31 = f32[32,32,128]{2,1,0:T(8,128)S(1)} all-to-all(f32[32,32,128]{2,1,0:T(8,128)S(1)} %broadcast_select_fusion.2), channel_id=1, replica_groups=mesh['row'=4,'col'=8] {'row','col'}, dimensions={0} | all-to-all | bytes 1048576 | tf_op jit(solution)/shard_map/all_to_all | solution.py:97
  574.9 38.8 %all-reduce.8.cloned.1.call-done = f32[2048,128]{0,1:T(8,128)} async-done(((f32[2048,128]{0,1:T(8,128)}), f32[2048,128]{0,1:T(8,128)}) %all-reduce.8.cloned.1.call-update) | async-done | bytes 1048592 | tf_op jit(solution)/shard_map/psum | solution.py:20
  613.7 39.2 %fusion.31 = f32[128,4096]{1,0:T(8,128)} fusion(f32[2048,128]{0,1:T(8,128)} %all-reduce.8.cloned.1.call-done, f32[4096,2048]{1,0:T(8,128)} %param.21), kind=kOutput, calls=%fused_computation.108 | convolution fusion | flops 12884901888 | bytes 36700160 | tf_op jit(solution)/shard_map/dot_general | solution.py:119
  655.6 4.1 collective-permute-done.8
  662.9 2.8 gather_fusion.8
  666.8 4.0 all-to-all-start.5
  670.8 42.8 %collective-permute-done.9 = f32[4096,128]{0,1:T(8,128)} collective-permute-done((f32[4096,128]{0,1:T(8,128)}, f32[4096,128]{0,1:T(8,128)}, u32[]{:S(2)}, u32[]{:S(2)}) %collective-permute-start.9) | collective-permute-done | bytes 2097184 | tf_op jit(solution)/shard_map/ppermute | solution.py:128
  713.6 3.8 add.209
  719.9 91.6 %collective-permute-done.11 = f32[8,64,128]{2,1,0:T(8,128)S(1)} collective-permute-done((f32[8,64,128]{2,1,0:T(8,128)S(1)}, f32[8,64,128]{2,1,0:T(8,128)S(1)}, u32[]{:S(2)}, u32[]{:S(2)}) %collective-permute-start.11) | collective-permute-done | bytes 262176 | tf_op jit(solution)/shard_map/ppermute | solution.py:15
  811.5 3.7 gather_fusion.11
  815.5 8.1 scatter_custom_fusion.2
  823.5 9.9 %fusion.3 = f32[8,512,128]{2,1,0:T(8,128)S(1)} fusion(f32[8,512,128]{2,1,0:T(8,128)S(1)} %fusion.20, f32[8,512,128]{2,1,0:T(8,128)} %bitcast.110, f32[8,512,512]{2,1,0:T(8,128)} %param.22), kind=kOutput, calls=%fused_computation.21 | convolution fusion | flops 3223322624 | bytes 14680064 | tf_op jit(solution)/shard_map/enm,emr->enr/dot_general | solution.py:133
  834.9 2.6 multiply_subtract_fusion
  (132 shorter events, 48.0 us)
Async XLA Ops:
  7.2 60.3 %all-reduce.4.cloned.1.call-start = ((), (), s32[]{:S(2)}) async-start(), calls=%async_computation.6 | async-start | bytes 2097152 | tf_op jit(solution)/shard_map/psum | solution.py:20
  10.1 2.5 copy-start.7
  10.1 2.5 copy-start.8
  10.1 5.5 copy-start.9
  10.1 6.9 copy-start.1
  19.9 6.9 copy-start.6
  20.9 19.0 %all-to-all-start = ((f32[32,32,128]{2,1,0:T(8,128)}), f32[32,32,128]{2,1,0:T(8,128)S(1)}, u32[]{:S(2)}, u32[]{:S(2)}) async-start(f32[32,32,128]{2,1,0:T(8,128)} %broadcast_select_fusion.8), calls=%async_computation | async-start | bytes 1048576 | tf_op jit(solution)/shard_map/all_to_all | solution.py:97
  106.6 1.6 copy-start.11
  109.3 12.6 %copy-start.10 = (s32[16384]{0:T(1024)S(1)}, s32[16384]{0:T(1024)}, u32[]{:S(2)}) copy-start(s32[16384]{0:T(1024)} %param.26) | copy-start | bytes 196612
  109.3 4.2 collective-permute-start
  115.1 51.2 %collective-permute-start.1 = (f32[4096,128]{0,1:T(8,128)}, f32[4096,128]{0,1:T(8,128)}, u32[]{:S(2)}, u32[]{:S(2)}) collective-permute-start(f32[4096,128]{0,1:T(8,128)} %add.193), channel_id=1, source_target_pairs={{0,2},{1,3},{2,0},{3,1},{4,6},{5,7},{6,4},{7,5},{8,10},{9,11},{10,... | collective-permute-start | bytes 6291464 | tf_op jit(solution)/shard_map/ppermute | solution.py:128
  116.6 59.3 %collective-permute-start.3 = (f32[8,64,128]{2,1,0:T(8,128)S(1)}, f32[8,64,128]{2,1,0:T(8,128)S(1)}, u32[]{:S(2)}, u32[]{:S(2)}) collective-permute-start(f32[8,64,128]{2,1,0:T(8,128)S(1)} %slice.98), channel_id=1, source_target_pairs={{0,1},{1,2},{2,3},{3,4},{4,5},{5,6},{6,7},{7,8},{8,9},{9,10},{10,1... | collective-permute-start | bytes 786440 | tf_op jit(solution)/shard_map/ppermute | solution.py:15
  126.7 53.0 %all-to-all-start.1 = ((f32[32,32,128]{2,1,0:T(8,128)}), f32[32,32,128]{2,1,0:T(8,128)S(1)}, u32[]{:S(2)}, u32[]{:S(2)}) async-start(f32[32,32,128]{2,1,0:T(8,128)} %broadcast_select_fusion.7), calls=%async_computation.1 | async-start | bytes 1048576 | tf_op jit(solution)/shard_map/all_to_all | solution.py:100
  132.7 42.4 %copy-start.12 = (s32[8,64]{1,0:T(8,128)S(1)}, s32[8,64]{1,0:T(8,128)}, u32[]{:S(2)}) copy-start(s32[8,64]{1,0:T(8,128)} %param.27) | copy-start | bytes 6148
  132.7 194.7 %all-reduce.6.cloned.1.call-start = ((), (), s32[]{:S(2)}) async-start(), calls=%async_computation.7 | async-start | bytes 2097152 | tf_op jit(solution)/shard_map/psum | solution.py:20
  170.1 92.5 %collective-permute-start.2 = (f32[4096,128]{0,1:T(8,128)}, f32[4096,128]{0,1:T(8,128)}, u32[]{:S(2)}, u32[]{:S(2)}) collective-permute-start(f32[4096,128]{0,1:T(8,128)} %add.194), channel_id=1, source_target_pairs={{0,4},{1,5},{2,6},{3,7},{4,0},{5,1},{6,2},{7,3},{8,12},{9,13},{10,... | collective-permute-start | bytes 6291464 | tf_op jit(solution)/shard_map/ppermute | solution.py:128
  199.0 232.7 %copy-start = (f32[8,512,128]{2,1,0:T(8,128)}, f32[8,512,128]{2,1,0:T(8,128)S(1)}, u32[]{:S(2)}) copy-start(f32[8,512,128]{2,1,0:T(8,128)S(1)} %fusion.21) | copy-start | bytes 6291460
  265.8 1.3 copy-start.4
  369.3 4.2 collective-permute-start.4
  375.0 52.2 %collective-permute-start.5 = (f32[4096,128]{0,1:T(8,128)}, f32[4096,128]{0,1:T(8,128)}, u32[]{:S(2)}, u32[]{:S(2)}) collective-permute-start(f32[4096,128]{0,1:T(8,128)} %add.202), channel_id=1, source_target_pairs={{0,2},{1,3},{2,0},{3,1},{4,6},{5,7},{6,4},{7,5},{8,10},{9,11},{10,... | collective-permute-start | bytes 6291464 | tf_op jit(solution)/shard_map/ppermute | solution.py:128
  380.5 148.5 %all-to-all-start.3 = ((f32[32,32,128]{2,1,0:T(8,128)}), f32[32,32,128]{2,1,0:T(8,128)S(1)}, u32[]{:S(2)}, u32[]{:S(2)}) async-start(f32[32,32,128]{2,1,0:T(8,128)} %broadcast_select_fusion.4), calls=%async_computation.3 | async-start | bytes 1048576 | tf_op jit(solution)/shard_map/all_to_all | solution.py:100
  384.5 229.2 %all-reduce.8.cloned.1.call-start = ((), (), s32[]{:S(2)}) async-start(), calls=%async_computation.8 | async-start | bytes 2097152 | tf_op jit(solution)/shard_map/psum | solution.py:20
  431.1 119.9 %collective-permute-start.6 = (f32[4096,128]{0,1:T(8,128)}, f32[4096,128]{0,1:T(8,128)}, u32[]{:S(2)}, u32[]{:S(2)}) collective-permute-start(f32[4096,128]{0,1:T(8,128)} %add.203), channel_id=1, source_target_pairs={{0,4},{1,5},{2,6},{3,7},{4,0},{5,1},{6,2},{7,3},{8,12},{9,13},{10,... | collective-permute-start | bytes 6291464 | tf_op jit(solution)/shard_map/ppermute | solution.py:128
  431.7 93.5 %collective-permute-start.7 = (f32[8,64,128]{2,1,0:T(8,128)S(1)}, f32[8,64,128]{2,1,0:T(8,128)S(1)}, u32[]{:S(2)}, u32[]{:S(2)}) collective-permute-start(f32[8,64,128]{2,1,0:T(8,128)S(1)} %slice.131), channel_id=1, source_target_pairs={{0,1},{1,2},{2,3},{3,4},{4,5},{5,6},{6,7},{7,8},{8,9},{9,10},{10,1... | collective-permute-start | bytes 786440 | tf_op jit(solution)/shard_map/ppermute | solution.py:15
  554.2 1.3 copy-start.2
  655.6 4.2 collective-permute-start.8
  661.3 52.2 %collective-permute-start.9 = (f32[4096,128]{0,1:T(8,128)}, f32[4096,128]{0,1:T(8,128)}, u32[]{:S(2)}, u32[]{:S(2)}) collective-permute-start(f32[4096,128]{0,1:T(8,128)} %add.208), channel_id=1, source_target_pairs={{0,2},{1,3},{2,0},{3,1},{4,6},{5,7},{6,4},{7,5},{8,10},{9,11},{10,... | collective-permute-start | bytes 6291464 | tf_op jit(solution)/shard_map/ppermute | solution.py:128
  666.8 148.5 %all-to-all-start.5 = ((f32[32,32,128]{2,1,0:T(8,128)}), f32[32,32,128]{2,1,0:T(8,128)S(1)}, u32[]{:S(2)}, u32[]{:S(2)}) async-start(f32[32,32,128]{2,1,0:T(8,128)} %broadcast_select_fusion.1), calls=%async_computation.5 | async-start | bytes 1048576 | tf_op jit(solution)/shard_map/all_to_all | solution.py:100
  717.4 117.5 %collective-permute-start.10 = (f32[4096,128]{0,1:T(8,128)}, f32[4096,128]{0,1:T(8,128)}, u32[]{:S(2)}, u32[]{:S(2)}) collective-permute-start(f32[4096,128]{0,1:T(8,128)} %add.209), channel_id=1, source_target_pairs={{0,4},{1,5},{2,6},{3,7},{4,0},{5,1},{6,2},{7,3},{8,12},{9,13},{10,... | collective-permute-start | bytes 6291464 | tf_op jit(solution)/shard_map/ppermute | solution.py:128
  718.0 93.5 %collective-permute-start.11 = (f32[8,64,128]{2,1,0:T(8,128)S(1)}, f32[8,64,128]{2,1,0:T(8,128)S(1)}, u32[]{:S(2)}, u32[]{:S(2)}) collective-permute-start(f32[8,64,128]{2,1,0:T(8,128)S(1)} %slice.133), channel_id=1, source_target_pairs={{0,1},{1,2},{2,3},{3,4},{4,5},{5,6},{6,7},{7,8},{8,9},{9,10},{10,1... | collective-permute-start | bytes 786440 | tf_op jit(solution)/shard_map/ppermute | solution.py:15
  823.5 11.4 %copy-start.3 = (f32[4096,128]{0,1:T(8,128)S(1)}, f32[4096,128]{0,1:T(8,128)}, u32[]{:S(2)}) copy-start(f32[4096,128]{0,1:T(8,128)} %copy-done.2) | copy-start | bytes 6291460
  833.6 1.3 copy-start.5
Sparse Core Ops, SparseCore 0:
  12.7 54.6 all-reduce.3
  268.3 59.0 all-reduce.5
  556.7 56.9 all-reduce.7
